TPU v7x, 32 devices: a whole 2x2x4 slice. The times are simulated.
32 devices in a mesh: grp: 2 (over y), wide: 8 (over z, x), narrow: 2 (over core).
Axes of the slice: x: 2, y: 2, z: 4, core: 2. Of those that a mesh axis runs over, the one named last changes fastest.
Arguments:
- node_latent: bfloat16 [5120, 512], P(('grp', 'wide', 'narrow')), parts along dimension 0, may hold values from -6 to 6
- fine_edges: bfloat16 [30720, 512], P(('grp', 'wide', 'narrow')), parts along dimension 0, may hold values from -6 to 6
- fine_senders: int32 [30720], P(('grp', 'wide', 'narrow')), parts along dimension 0, may hold values from 0 to 2559, as said below
- fine_receivers: int32 [30720], P(('grp', 'wide', 'narrow')), parts along dimension 0, may hold values from 0 to 2559, as said below
- coarse_edges: bfloat16 [1024, 512], P(('grp', 'wide', 'narrow')), parts along dimension 0, may hold values from -6 to 6
- coarse_senders: int32 [1024], P(('grp', 'wide', 'narrow')), parts along dimension 0, may hold values from 0 to 2403, as said below
- coarse_receivers: int32 [1024], P(('grp', 'wide', 'narrow')), parts along dimension 0, may hold values from 0 to 2403, as said below
- edge_weight_in: bfloat16 [1536, 512], replicated, may hold values from -0.15625 to 0.15625
- edge_bias: float32 [512], replicated, may hold values from -3 to 3
- edge_weight_out: bfloat16 [512, 512], replicated, may hold values from -0.25 to 0.25
- edge_gain: float32 [512], replicated, may hold values from 0.5 to 1.5
- edge_shift: float32 [512], replicated, may hold values from -2 to 2
- node_weight_in: bfloat16 [1024, 512], replicated, may hold values from -0.1875 to 0.1875
- node_bias: float32 [512], replicated, may hold values from -3 to 3
- node_weight_out: bfloat16 [512, 512], replicated, may hold values from -0.25 to 0.25
- node_gain: float32 [512], replicated, may hold values from 0.5 to 1.5
- node_shift: float32 [512], replicated, may hold values from -2 to 2
Outputs:
- node_out: bfloat16 [5120, 512], P(('grp', 'wide', 'narrow')), parts along dimension 0
There are 2 independent parts, one for each index of `grp`. A program takes and returns all parts, laid end to end along the dimension named above; an argument that names none is the same for every part. Nothing has to cross between parts.
Inputs may be any that keep to these rules, and one draw needn't show every extreme that they name: `fine_receivers`: node v belongs to device v // 160 (devices numbered wide index times 2 plus narrow index) and to patch v // 320. Each block of 960 fine edges belongs to one device, in order, and its receivers are that device's nodes. `fine_senders`: the sender of a fine edge lies in the receiver's patch p, or is a boundary node (v % 160 >= 140) of a device of patch p - 1 or p + 1, modulo 8. `coarse_receivers`: coarse nodes are the nodes v with v % 160 < 4. Each block of 32 coarse edges belongs to one device, in order, and its receivers are that device's coarse nodes; each coarse node receives at least one. `coarse_senders`: every coarse sender is a coarse node, on any device.
All inputs are finite; a program needn't handle non-finite values.
Results may differ from a plain program's by a relative error of at most 0.0053.
Values may be sent and summed in bfloat16 or wider, within the bound.
No kernel may reach another device: no remote copies, remote signals or barrier semaphores. Data moves between devices by JAX's collectives and lax.ppermute only.
A program may use at most 64 MiB of HBM per device.

v0:
```python
import jax
import jax.numpy as jnp
from jax import lax
from jax.sharding import PartitionSpec as P

COARSE_DEV = 4


def with_halo(shard, sides, width):
    for axis, dim in sides:
        devices, length = (lax.axis_size(axis), shard.shape[dim])
        up = [(i, (i + 1) % devices) for i in range(devices)]
        down = [(j, i) for i, j in up]
        last = lax.slice_in_dim(shard, length - width, length, axis=dim)
        first = lax.slice_in_dim(shard, 0, width, axis=dim)
        before = lax.ppermute(last, axis, up)
        after = lax.ppermute(first, axis, down)
        shard = jnp.concatenate([before, shard, after], axis=dim)
    return shard


def layer_norm(values, gain_vector, shift_vector):
    center = values - jnp.mean(values, axis=-1, keepdims=True)
    spread = jnp.mean(center * center, axis=-1, keepdims=True)
    return center * lax.rsqrt(spread + 1e-05) * gain_vector + shift_vector


def run_mlp(preact, weight_out, gain_vector, shift_vector):
    hidden = jax.nn.silu(preact).astype(jnp.bfloat16)
    output = jnp.dot(hidden, weight_out, preferred_element_type=jnp.float32)
    return layer_norm(output, gain_vector, shift_vector)


def shards(
    node_latent,
    fine_edges,
    fine_senders,
    fine_receivers,
    coarse_edges,
    coarse_senders,
    coarse_receivers,
    edge_weight_in,
    edge_bias,
    edge_weight_out,
    edge_gain,
    edge_shift,
    node_weight_in,
    node_bias,
    node_weight_out,
    node_gain,
    node_shift,
):
    node_count, latent_width = node_latent.shape
    halo_count = node_count // 8
    halo_first = node_count - halo_count
    n_narrow = lax.axis_size("narrow")
    wide_index = lax.axis_index("wide")
    narrow_index = lax.axis_index("narrow")
    device = wide_index * n_narrow + narrow_index
    patch_size = node_count * n_narrow
    patch_start = wide_index * patch_size
    w_edge = edge_weight_in[:latent_width]
    w_send = edge_weight_in[latent_width : 2 * latent_width]
    w_recv = edge_weight_in[2 * latent_width :]
    patch_rows = lax.all_gather(node_latent, "narrow", axis=0, tiled=True)
    edge_rows = patch_rows.reshape(n_narrow, node_count, latent_width)[:, halo_first:].reshape(
        -1, latent_width
    )
    halves = jnp.arange(n_narrow * halo_count, dtype=jnp.int32) // halo_count
    within_halo = jnp.arange(n_narrow * halo_count, dtype=jnp.int32) % halo_count
    edge_ids = patch_start + halves * node_count + halo_first + within_halo
    rows_near, ids_near = (
        with_halo(edge_rows[None], (("wide", 0),), 1),
        with_halo(edge_ids[None], (("wide", 0),), 1),
    )
    remote_rows = jnp.concatenate([rows_near[0], rows_near[2]], axis=0)
    remote_ids = jnp.concatenate([ids_near[0], ids_near[2]], axis=0)
    node_proj = jnp.dot(node_latent, w_recv, preferred_element_type=jnp.float32)
    patch_proj = jnp.dot(patch_rows, w_send, preferred_element_type=jnp.float32)
    remote_proj = jnp.dot(remote_rows, w_send, preferred_element_type=jnp.float32)
    offsets = fine_senders - patch_start
    inside = (offsets >= 0) & (offsets < patch_size)
    inner_pos = jnp.clip(offsets, 0, patch_size - 1)
    matches = fine_senders[:, None] == remote_ids[None, :]
    positions = jnp.arange(remote_ids.shape[0], dtype=jnp.int32)
    outer_pos = jnp.sum(jnp.where(matches, positions[None, :], 0), axis=1)
    sender_term = jnp.where(inside[:, None], patch_proj[inner_pos], remote_proj[outer_pos])
    local_recv = fine_receivers - device * node_count
    fine_pre = (
        jnp.dot(fine_edges, w_edge, preferred_element_type=jnp.float32)
        + sender_term
        + node_proj[local_recv]
    )
    table_slots = coarse_senders // node_count * COARSE_DEV + coarse_senders % node_count
    shard_rows = lax.all_gather(node_latent[:COARSE_DEV], ("wide", "narrow"), axis=0, tiled=True)
    wanted = jnp.arange(shard_rows.shape[0], dtype=jnp.int32)
    selector = (table_slots[:, None] == wanted[None, :]).astype(jnp.bfloat16)
    coarse_rows = jnp.dot(selector, shard_rows, preferred_element_type=jnp.float32).astype(
        jnp.bfloat16
    )
    coarse_local = coarse_receivers - device * node_count
    coarse_pre = jnp.dot(coarse_edges, w_edge, preferred_element_type=jnp.float32)
    coarse_pre = (
        coarse_pre
        + jnp.dot(coarse_rows, w_send, preferred_element_type=jnp.float32)
        + node_proj[coarse_local]
    )
    preact = jnp.concatenate([fine_pre, coarse_pre], axis=0) + edge_bias
    messages = run_mlp(preact, edge_weight_out, edge_gain, edge_shift).astype(jnp.bfloat16)
    receivers_all = jnp.concatenate([local_recv, coarse_local], axis=0)
    node_slots = jnp.arange(node_count, dtype=jnp.int32)
    incidence = (node_slots[:, None] == receivers_all[None, :]).astype(jnp.bfloat16)
    summed = jnp.dot(incidence, messages, preferred_element_type=jnp.float32).astype(jnp.bfloat16)
    node_pre = jnp.dot(
        node_latent, node_weight_in[:latent_width], preferred_element_type=jnp.float32
    )
    node_pre = node_pre + jnp.dot(
        summed, node_weight_in[latent_width:], preferred_element_type=jnp.float32
    )
    node_pre = node_pre + node_bias
    node_update = run_mlp(node_pre, node_weight_out, node_gain, node_shift)
    return (node_latent.astype(jnp.float32) + node_update).astype(jnp.bfloat16)


def solution(mesh):
    return jax.shard_map(
        shards,
        mesh=mesh,
        in_specs=(
            P(("grp", "wide", "narrow"), None),
            P(("grp", "wide", "narrow"), None),
            P(("grp", "wide", "narrow")),
            P(("grp", "wide", "narrow")),
            P(("grp", "wide", "narrow"), None),
            P(("grp", "wide", "narrow")),
            P(("grp", "wide", "narrow")),
            P(),
            P(),
            P(),
            P(),
            P(),
            P(),
            P(),
            P(),
            P(),
            P(),
        ),
        out_specs=P(("grp", "wide", "narrow"), None),
        check_vma=False,
    )
```

profile of v0, /device:TPU:0, one launch (start us, length us, event | category | flops | bytes accessed | tf_op | source)
XLA Modules:
  0.0 80.6 jit_solution(10833074330517770571)
XLA Ops:
  0.6 3.0 %collective-permute-start.2 = (s32[1,40]{1,0:T(1,128)}, s32[1,40]{1,0:T(1,128)}, u32[]{:S(2)}, u32[]{:S(2)}) collective-permute-start(s32[1,40]{1,0:T(1,128)} %fusion.32), channel_id=1, source_target_pairs={{0,2},{2,4},{4,6},{6,8},{8,10},{10,12},{12,14},{14,0},{1,3},{3,5},... | collective-permute-start | bytes 488 | tf_op jit(solution)/shard_map/ppermute | solution.py:16
  3.5 3.0 %collective-permute-start.3 = (s32[1,40]{1,0:T(1,128)}, s32[1,40]{1,0:T(1,128)}, u32[]{:S(2)}, u32[]{:S(2)}) collective-permute-start(s32[1,40]{1,0:T(1,128)} %fusion.32), channel_id=1, source_target_pairs={{2,0},{4,2},{6,4},{8,6},{10,8},{12,10},{14,12},{0,14},{3,1},{5,3},... | collective-permute-start | bytes 488 | tf_op jit(solution)/shard_map/ppermute | solution.py:17
  6.6 2.2 %all_gather.6 = bf16[320,512]{1,0:T(8,128)(2,1)S(1)} all-gather(bf16[160,512]{1,0:T(8,128)(2,1)} %param.17), channel_id=1, replica_groups=mesh['grp'=2,'wide'=8,'narrow'=2] {'narrow'}, dimensions={0}, use_global_device_ids=true | all-gather | bytes 491520 | tf_op jit(solution)/shard_map/all_gather | solution.py:65
  8.8 0.7 copy-done.4
  9.6 0.6 broadcast_in_dim_reshape.3
  10.2 4.7 %collective-permute-start.1 = (bf16[1,40,512]{2,1,0:T(8,128)(2,1)}, bf16[1,40,512]{2,1,0:T(8,128)(2,1)}, u32[]{:S(2)}, u32[]{:S(2)}) collective-permute-start(bf16[1,40,512]{2,1,0:T(8,128)(2,1)} %broadcast_in_dim_reshape.3), channel_id=1, source_target_pairs={{2,0},{4,2},{6,4},{8,6},{10,8},{12,10},{14,12},{0,14},{3,1},{5,3},... | collective-permute-start | bytes 122888 | tf_op jit(solution)/shard_map/ppermute | solution.py:17
  14.9 1.4 %fusion.10 = f32[160,512]{1,0:T(8,128)S(1)} fusion(bf16[160,512]{1,0:T(8,128)(2,1)} %param.17, bf16[1536,512]{1,0:T(8,128)(2,1)} %param.24), kind=kOutput, calls=%fused_computation.21 | convolution fusion | flops 83886080 | bytes 1015808 | tf_op jit(solution)/shard_map/dot_general | solution.py:78
  16.3 1.3 %fusion.21 = f32[320,512]{1,0:T(8,128)S(1)} fusion(bf16[320,512]{1,0:T(8,128)(2,1)} %copy-done.4, bf16[1536,512]{1,0:T(8,128)(2,1)S(1)} %copy-done.2), kind=kOutput, calls=%fused_computation.32 | convolution fusion | flops 167772160 | bytes 1507328 | tf_op jit(solution)/shard_map/dot_general | solution.py:79
  17.6 0.6 compare_select_fusion.2
  18.8 1.3 %slice_bitcast_fusion = bf16[1,4,512]{2,1,0:T(4,128)(2,1)} fusion(bf16[160,512]{1,0:T(8,128)(2,1)} %param.17), kind=kLoop, calls=%fused_computation.53 | loop fusion | bytes 8192
  20.1 0.7 pad_clamp_fusion.3
  20.8 2.0 %fusion.16 = f32[960,512]{1,0:T(8,128)} fusion(bf16[960,512]{1,0:T(8,128)(2,1)S(1)} %copy-done, bf16[1536,512]{1,0:T(8,128)(2,1)S(1)} %copy-done.2), kind=kOutput, calls=%fused_computation.27 | convolution fusion | flops 503316480 | bytes 3473408 | tf_op jit(solution)/shard_map/dot_general | solution.py:90
  22.7 1.2 %compare_select_fusion.3 = (s32[32]{0:T(128)S(1)}, s32[32]{0:T(128)}) fusion(s32[32]{0:T(128)} %param.23, s32[]{:T(128)S(6)} %mul.76), kind=kLoop, calls=%fused_computation.55 | loop fusion | flops 128 | bytes 388 | tf_op jit(solution)/shard_map/select_n | solution.py:106
  23.9 0.6 pad_clamp_fusion
  24.5 18.7 %all-gather = bf16[16,4,512]{2,1,0:T(4,128)(2,1)} all-gather(bf16[1,4,512]{2,1,0:T(4,128)(2,1)S(1)} %copy-done.8), channel_id=1, replica_groups=mesh['grp'=2,'wide'=8,'narrow'=2] {'wide','narrow'}, dimensions={0}, use_global_device_ids=true | all-gather | bytes 69632 | tf_op jit(solution)/shard_map/all_gather | solution.py:95
  43.2 1.5 %reshape.147 = bf16[64,512]{1,0:T(8,128)(2,1)} reshape(bf16[16,4,512]{2,1,0:T(4,128)(2,1)} %all-gather) | data formatting | bytes 131072
  44.7 1.6 %fusion.14 = f32[32,512]{1,0:T(8,128)} fusion(bf16[32,512]{1,0:T(8,128)(2,1)} %param.21, bf16[1536,512]{1,0:T(8,128)(2,1)S(1)} %copy-done.2), kind=kOutput, calls=%fused_computation.25 | convolution fusion | flops 16777216 | bytes 622592 | tf_op jit(solution)/shard_map/dot_general | solution.py:102
  46.2 1.2 %fusion.33 = s32[32]{0:T(128)} fusion(s32[32]{0:T(128)} %param.22), kind=kLoop, calls=%fused_computation.67 | loop fusion | flops 448 | bytes 256 | tf_op jit(solution)/shard_map/add | solution.py:94
  47.5 2.1 %fusion.12 = f32[160,512]{1,0:T(8,128)} fusion(bf16[160,512]{1,0:T(8,128)(2,1)} %param.17, bf16[1024,512]{1,0:T(8,128)(2,1)} %param.29), kind=kOutput, calls=%fused_computation.23 | convolution fusion | flops 83886080 | bytes 1015808 | tf_op jit(solution)/shard_map/dot_general | solution.py:114
  49.6 1.3 %gather_fusion.3 = f32[32,512]{1,0:T(8,128)} fusion(f32[160,512]{1,0:T(8,128)S(1)} %fusion.10, s32[1024]{0:T(1024)} %pad_clamp_fusion), kind=kCustom, calls=%fused_computation.3 | custom fusion | bytes 131200 | tf_op jit(solution)/shard_map/gather | solution.py:106
  50.9 1.9 %fusion.1 = f32[32,512]{1,0:T(8,128)} fusion(f32[32,512]{1,0:T(8,128)} %gather_fusion.3, f32[32,512]{1,0:T(8,128)} %fusion.14, bf16[64,512]{1,0:T(8,128)(2,1)} %reshape.147, bf16[1536,512]{1,0:T(8,128)(2,1)S(1)} %copy-done.2, s32[32]{0:T(128)} %fusion.33), kind=kOutput, calls=%fused_computation.13 | convolution fusion | flops 18925568 | bytes 786560 | tf_op jit(solution)/shard_map/dot_general | solution.py:105
  52.8 0.7 pad_add_fusion
  53.5 4.9 %gather_fusion.2 = f32[960,512]{1,0:T(8,128)} fusion(f32[160,512]{1,0:T(8,128)S(1)} %fusion.10, s32[1024]{0:T(1024)S(1)} %pad_clamp_fusion.1), kind=kCustom, calls=%fused_computation.2 | custom fusion | bytes 3936000 | tf_op jit(solution)/shard_map/gather | solution.py:92
  58.4 4.8 %gather_fusion = f32[960,512]{1,0:T(8,128)} fusion(f32[320,512]{1,0:T(8,128)S(1)} %fusion.21, s32[1024]{0:T(1024)S(1)} %pad_clamp_fusion.3), kind=kCustom, calls=%fused_computation | custom fusion | bytes 3936000 | tf_op jit(solution)/shard_map/gather | solution.py:87
  63.2 0.7 pad_add_fusion.1
  64.1 1.3 %fusion.19 = f32[80,512]{1,0:T(8,128)S(1)} fusion(bf16[1536,512]{1,0:T(8,128)(2,1)} %param.24, bf16[40,512]{1,0:T(8,128)(2,1)} %bitcast.2, bf16[40,512]{1,0:T(8,128)(2,1)} %bitcast.1), kind=kOutput, calls=%fused_computation.30 | convolution fusion | flops 42106880 | bytes 770048 | tf_op jit(solution)/shard_map/dot_general | solution.py:80
  65.5 4.8 %gather_fusion.1 = f32[960,512]{1,0:T(8,128)} fusion(f32[80,512]{1,0:T(8,128)S(1)} %fusion.19, s32[1024]{0:T(1024)S(1)} %pad_clamp_fusion.2), kind=kCustom, calls=%fused_computation.1 | custom fusion | bytes 3936000 | tf_op jit(solution)/shard_map/gather | solution.py:87
  70.3 3.2 %add_add_fusion = f32[960,512]{1,0:T(8,128)S(1)} fusion(f32[960,512]{1,0:T(8,128)} %gather_fusion.2, f32[960,512]{1,0:T(8,128)S(1)} %copy-done.1, f32[960,512]{1,0:T(8,128)} %gather_fusion, f32[960,512]{1,0:T(8,128)} %gather_fusion.1, pred[960]{0:T(1024)(128)(4,1)S(1)} %copy-done.9), kind=kLoop, calls=%fused_computation.8 | loop fusion | flops 1474560 | bytes 9831360 | tf_op jit(solution)/shard_map/add | solution.py:90
  73.6 0.8 fusion.40
  75.4 2.7 %multiply_convert_fusion.2 = bf16[160,512]{1,0:T(8,128)(2,1)} fusion(f32[160,512]{1,0:T(8,128)S(1)} %copy-done.5, bf16[1024,512]{1,0:T(8,128)(2,1)} %param.29, f32[992,512]{1,0:T(8,128)S(1)} %get-tuple-element.10, f32[512]{0:T(512)S(1)} %copy-done.15, f32[512]{0:T(512)S(1)} %copy-done.16, f32[992]{0:T(1024)S(1)} %add_rsqrt_fusion, ...), kind=kOutput, calls=%fused_computation.36 | convolution fusion | flops 249768960 | bytes 3065472 | tf_op jit(solution)/shard_map/dot_general | solution.py:117
  78.0 1.5 %fusion.41 = (f32[160]{0:T(256)S(1)}, f32[160,512]{1,0:T(8,128)S(1)}) fusion(bf16[160,512]{1,0:T(8,128)(2,1)} %multiply_convert_fusion.2, bf16[512,512]{1,0:T(8,128)(2,1)} %param.31), kind=kOutput, calls=%fused_computation.78 | convolution fusion | flops 83967840 | bytes 1016448 | tf_op jit(solution)/shard_map/dot_general | solution.py:30
  79.8 0.8 %add_convert_fusion.3 = bf16[160,512]{1,0:T(8,128)(2,1)} fusion(bf16[160,512]{1,0:T(8,128)(2,1)S(1)} %copy-done.3, f32[160,512]{1,0:T(8,128)S(1)} %get-tuple-element.12, f32[512]{0:T(512)S(1)} %copy-done.11, f32[512]{0:T(512)S(1)} %copy-done.12, f32[160]{0:T(256)S(1)} %add_rsqrt_fusion.1, f32[160]{0:T(256)S(1)} %broadcast_multiply_fusion.1), kind=kLoop, calls=%fused_computation.34 | loop fusion | flops 573440 | bytes 660736 | tf_op jit(solution)/shard_map/convert_element_type | solution.py:122
  (54 shorter events, 2.4 us)
Async XLA Ops:
  0.0 20.7 %copy-start = (bf16[960,512]{1,0:T(8,128)(2,1)S(1)}, bf16[960,512]{1,0:T(8,128)(2,1)}, u32[]{:S(2)}) copy-start(bf16[960,512]{1,0:T(8,128)(2,1)} %param.18) | copy-start | bytes 2949124
  0.0 16.3 %copy-start.2 = (bf16[1536,512]{1,0:T(8,128)(2,1)S(1)}, bf16[1536,512]{1,0:T(8,128)(2,1)}, u32[]{:S(2)}) copy-start(bf16[1536,512]{1,0:T(8,128)(2,1)} %param.24) | copy-start | bytes 4718596
  0.0 17.6 %copy-start.7 = (s32[960]{0:T(1024)S(1)}, s32[960]{0:T(1024)}, u32[]{:S(2)}) copy-start(s32[960]{0:T(1024)} %param.19) | copy-start | bytes 11524
  0.0 20.0 %copy-start.10 = (s32[960]{0:T(1024)S(1)}, s32[960]{0:T(1024)}, u32[]{:S(2)}) copy-start(s32[960]{0:T(1024)} %param.20) | copy-start | bytes 11524
  0.6 62.6 %collective-permute-start.2 = (s32[1,40]{1,0:T(1,128)}, s32[1,40]{1,0:T(1,128)}, u32[]{:S(2)}, u32[]{:S(2)}) collective-permute-start(s32[1,40]{1,0:T(1,128)} %fusion.32), channel_id=1, source_target_pairs={{0,2},{2,4},{4,6},{6,8},{8,10},{10,12},{12,14},{14,0},{1,3},{3,5},... | collective-permute-start | bytes 488 | tf_op jit(solution)/shard_map/ppermute | solution.py:16
  3.5 59.7 %collective-permute-start.3 = (s32[1,40]{1,0:T(1,128)}, s32[1,40]{1,0:T(1,128)}, u32[]{:S(2)}, u32[]{:S(2)}) collective-permute-start(s32[1,40]{1,0:T(1,128)} %fusion.32), channel_id=1, source_target_pairs={{2,0},{4,2},{6,4},{8,6},{10,8},{12,10},{14,12},{0,14},{3,1},{5,3},... | collective-permute-start | bytes 488 | tf_op jit(solution)/shard_map/ppermute | solution.py:17
  8.8 0.7 copy-start.4
  10.2 53.9 %collective-permute-start = (bf16[1,40,512]{2,1,0:T(8,128)(2,1)}, bf16[1,40,512]{2,1,0:T(8,128)(2,1)}, u32[]{:S(2)}, u32[]{:S(2)}) collective-permute-start(bf16[1,40,512]{2,1,0:T(8,128)(2,1)} %broadcast_in_dim_reshape.3), channel_id=1, source_target_pairs={{0,2},{2,4},{4,6},{6,8},{8,10},{10,12},{12,14},{14,0},{1,3},{3,5},... | collective-permute-start | bytes 122888 | tf_op jit(solution)/shard_map/ppermute | solution.py:16
  10.2 53.9 %collective-permute-start.1 = (bf16[1,40,512]{2,1,0:T(8,128)(2,1)}, bf16[1,40,512]{2,1,0:T(8,128)(2,1)}, u32[]{:S(2)}, u32[]{:S(2)}) collective-permute-start(bf16[1,40,512]{2,1,0:T(8,128)(2,1)} %broadcast_in_dim_reshape.3), channel_id=1, source_target_pairs={{2,0},{4,2},{6,4},{8,6},{10,8},{12,10},{14,12},{0,14},{3,1},{5,3},... | collective-permute-start | bytes 122888 | tf_op jit(solution)/shard_map/ppermute | solution.py:17
  20.0 4.5 %copy-start.8 = (bf16[1,4,512]{2,1,0:T(4,128)(2,1)S(1)}, bf16[1,4,512]{2,1,0:T(4,128)(2,1)}, u32[]{:S(2)}) copy-start(bf16[1,4,512]{2,1,0:T(4,128)(2,1)} %slice_bitcast_fusion) | copy-start | bytes 12292
  65.4 4.9 %copy-start.1 = (f32[960,512]{1,0:T(8,128)S(1)}, f32[960,512]{1,0:T(8,128)}, u32[]{:S(2)}) copy-start(f32[960,512]{1,0:T(8,128)} %fusion.16) | copy-start | bytes 5898244
  65.4 4.9 %copy-start.9 = (pred[960]{0:T(1024)(128)(4,1)S(1)}, pred[960]{0:T(1024)(128)(4,1)}, u32[]{:S(2)}) copy-start(pred[960]{0:T(1024)(128)(4,1)} %compare_and_fusion) | copy-start | bytes 2884
  70.3 3.2 %copy-start.6 = (f32[32,512]{1,0:T(8,128)S(1)}, f32[32,512]{1,0:T(8,128)}, u32[]{:S(2)}) copy-start(f32[32,512]{1,0:T(8,128)} %fusion.1) | copy-start | bytes 196612
  70.3 3.2 %copy-start.13 = (bf16[512,512]{1,0:T(8,128)(2,1)S(1)}, bf16[512,512]{1,0:T(8,128)(2,1)}, u32[]{:S(2)}) copy-start(bf16[512,512]{1,0:T(8,128)(2,1)} %param.26) | copy-start | bytes 1572868
  70.3 3.2 %copy-start.14 = (f32[512]{0:T(512)S(1)}, f32[512]{0:T(512)}, u32[]{:S(2)}) copy-start(f32[512]{0:T(512)} %param.25) | copy-start | bytes 6148
  74.4 1.0 %copy-start.5 = (f32[160,512]{1,0:T(8,128)S(1)}, f32[160,512]{1,0:T(8,128)}, u32[]{:S(2)}) copy-start(f32[160,512]{1,0:T(8,128)} %fusion.12) | copy-start | bytes 983044
  74.4 1.0 %copy-start.15 = (f32[512]{0:T(512)S(1)}, f32[512]{0:T(512)}, u32[]{:S(2)}) copy-start(f32[512]{0:T(512)} %param.28) | copy-start | bytes 6148
  74.4 1.0 %copy-start.16 = (f32[512]{0:T(512)S(1)}, f32[512]{0:T(512)}, u32[]{:S(2)}) copy-start(f32[512]{0:T(512)} %param.27) | copy-start | bytes 6148
  74.4 1.0 %copy-start.17 = (f32[512]{0:T(512)S(1)}, f32[512]{0:T(512)}, u32[]{:S(2)}) copy-start(f32[512]{0:T(512)} %param.30) | copy-start | bytes 6148
  75.3 4.4 %copy-start.3 = (bf16[160,512]{1,0:T(8,128)(2,1)S(1)}, bf16[160,512]{1,0:T(8,128)(2,1)}, u32[]{:S(2)}) copy-start(bf16[160,512]{1,0:T(8,128)(2,1)} %param.17) | copy-start | bytes 491524
  75.4 4.4 %copy-start.11 = (f32[512]{0:T(512)S(1)}, f32[512]{0:T(512)}, u32[]{:S(2)}) copy-start(f32[512]{0:T(512)} %param.33) | copy-start | bytes 6148
  75.4 4.4 %copy-start.12 = (f32[512]{0:T(512)S(1)}, f32[512]{0:T(512)}, u32[]{:S(2)}) copy-start(f32[512]{0:T(512)} %param.32) | copy-start | bytes 6148
where the time goes:
time: 81.2 us; the launch traced here: 80.6 us
  blocking collectives  20.9 us (26%)
  local copies, waits for them, and re-layouts  20.6 us (25%)
  matrix products  16.4 us (20%)
  other arithmetic  11.6 us (14%)
  starting transfers between devices  10.7 us (13%)
    all_gather x1, blocking collectives, shards(): lax.all_gather(node_latent[:COARSE_DEV], ('wide', 'narrow'), axis=0, tile...  18.7 us
    ppermute x2, starting transfers between devices, with_halo(): after = lax.ppermute(first, axis, down)  7.76 us
    gather x1, local copies, waits for them, and re-layouts, shards(): node_proj[local_recv]  4.86 us
    gather x1, local copies, waits for them, and re-layouts, shards(): remote_proj[outer_pos]  4.84 us
    gather x1, local copies, waits for them, and re-layouts, shards(): patch_proj[inner_pos]  4.82 us
    unnamed x38, local copies, waits for them, and re-layouts  4.08 us
    add x1, other arithmetic, shards(): jnp.dot(fine_edges, w_edge, preferred_element_type=jnp.float32)  3.19 us
    ppermute x2, starting transfers between devices, with_halo(): before = lax.ppermute(last, axis, up)  2.98 us
  transfers between devices with their start and end apart: 4, of which 0 were waited for; matrix products, arithmetic and copies ran while one was open for 39% of the time, Pallas kernels for 0%

commit v1 on v0

--- a/solution.py
+++ b/solution.py
@@ -92,7 +92,25 @@
         + node_proj[local_recv]
     )
     table_slots = coarse_senders // node_count * COARSE_DEV + coarse_senders % node_count
-    shard_rows = lax.all_gather(node_latent[:COARSE_DEV], ("wide", "narrow"), axis=0, tiled=True)
+    x = node_latent[:COARSE_DEV]
+    ways, here, step = (
+        lax.axis_size(("wide", "narrow")),
+        lax.axis_index(("wide", "narrow")),
+        x.shape[0],
+    )
+    line, have = (x, 1)
+    while have < ways:
+        line = jnp.concatenate(
+            [
+                line,
+                lax.ppermute(
+                    line, ("wide", "narrow"), [(d, (d - have) % ways) for d in range(ways)]
+                ),
+            ],
+            axis=0,
+        )
+        have = 2 * have
+    shard_rows = jnp.roll(line, here * step, axis=0)
     wanted = jnp.arange(shard_rows.shape[0], dtype=jnp.int32)
     selector = (table_slots[:, None] == wanted[None, :]).astype(jnp.bfloat16)
     coarse_rows = jnp.dot(selector, shard_rows, preferred_element_type=jnp.float32).astype(

time: 81.2 us -> 74.5 us (0.917)
  the two profiles are of different devices: /device:TPU:0 before, /device:TPU:10 now
where the time goes in v1:
time: 74.5 us; the launch traced here: 73.8 us
  local copies, waits for them, and re-layouts  19.4 us (26%)
  matrix products  16.4 us (22%)
  other arithmetic  15.2 us (20%)
  starting transfers between devices  15.1 us (20%)
  waiting for transfers between devices  5.12 us (7%)
  blocking collectives  2.24 us (3%)
    ppermute x4, starting transfers between devices, shards(): lax.ppermute(line, ('wide', 'narrow'), [(d, (d - have) % ways) for d in r...  10.6 us
    ppermute x4, waiting for transfers between devices, shards(): lax.ppermute(line, ('wide', 'narrow'), [(d, (d - have) % ways) for d in r...  5.11 us
    gather x1, local copies, waits for them, and re-layouts, shards(): node_proj[local_recv]  5.08 us
    gather x1, local copies, waits for them, and re-layouts, shards(): remote_proj[outer_pos]  4.85 us
    gather x1, local copies, waits for them, and re-layouts, shards(): patch_proj[inner_pos]  4.83 us
    add x1, other arithmetic, shards(): jnp.dot(fine_edges, w_edge, preferred_element_type=jnp.float32)  4.43 us
    ppermute x2, starting transfers between devices, with_halo(): before = lax.ppermute(last, axis, up)  3.99 us
    dot_general x2, matrix products, run_mlp(): output = jnp.dot(hidden, weight_out, preferred_element_type=jnp.float32)  3.93 us
  transfers between devices with their start and end apart: 8, of which 2 were waited for; matrix products, arithmetic and copies ran while one was open for 51% of the time, Pallas kernels for 0%

profile of v1, /device:TPU:10, one launch (start us, length us, event | category | flops | bytes accessed | tf_op | source)
XLA Modules:
  0.0 73.8 jit_solution(12775325216390493936)
XLA Ops:
  0.5 1.5 %collective-permute-start.2 = (s32[1,40]{1,0:T(1,128)}, s32[1,40]{1,0:T(1,128)}, u32[]{:S(2)}, u32[]{:S(2)}) collective-permute-start(s32[1,40]{1,0:T(1,128)} %fusion.34), channel_id=1, source_target_pairs={{0,2},{2,4},{4,6},{6,8},{8,10},{10,12},{12,14},{14,0},{1,3},{3,5},... | collective-permute-start | bytes 488 | tf_op jit(solution)/shard_map/ppermute | solution.py:16
  2.6 2.2 %all_gather.3 = bf16[320,512]{1,0:T(8,128)(2,1)S(1)} all-gather(bf16[160,512]{1,0:T(8,128)(2,1)} %param.17), channel_id=1, replica_groups=mesh['grp'=2,'wide'=8,'narrow'=2] {'narrow'}, dimensions={0}, use_global_device_ids=true | all-gather | bytes 491520 | tf_op jit(solution)/shard_map/all_gather | solution.py:65
  4.8 0.7 copy-done.5
  6.2 2.4 %collective-permute-start = (bf16[1,40,512]{2,1,0:T(8,128)(2,1)}, bf16[1,40,512]{2,1,0:T(8,128)(2,1)}, u32[]{:S(2)}, u32[]{:S(2)}) collective-permute-start(bf16[1,40,512]{2,1,0:T(8,128)(2,1)} %broadcast_in_dim_reshape.3), channel_id=1, source_target_pairs={{0,2},{2,4},{4,6},{6,8},{8,10},{10,12},{12,14},{14,0},{1,3},{3,5},... | collective-permute-start | bytes 122888 | tf_op jit(solution)/shard_map/ppermute | solution.py:16
  8.6 0.7 slice.26
  9.3 1.1 %collective-permute-start.4 = (bf16[4,512]{1,0:T(4,128)(2,1)S(1)}, bf16[4,512]{1,0:T(4,128)(2,1)S(1)}, u32[]{:S(2)}, u32[]{:S(2)}) collective-permute-start(bf16[4,512]{1,0:T(4,128)(2,1)S(1)} %slice.26), channel_id=1, source_target_pairs={{0,15},{1,0},{2,1},{3,2},{4,3},{5,4},{6,5},{7,6},{8,7},{9,8},{10,9... | collective-permute-start | bytes 12296 | tf_op jit(solution)/shard_map/ppermute | solution.py:106
  10.4 1.4 %fusion.10 = f32[160,512]{1,0:T(8,128)S(1)} fusion(bf16[160,512]{1,0:T(8,128)(2,1)} %param.17, bf16[1536,512]{1,0:T(8,128)(2,1)} %param.24), kind=kOutput, calls=%fused_computation.21 | convolution fusion | flops 83886080 | bytes 1015808 | tf_op jit(solution)/shard_map/dot_general | solution.py:78
  11.8 1.3 %fusion.21 = f32[320,512]{1,0:T(8,128)S(1)} fusion(bf16[320,512]{1,0:T(8,128)(2,1)} %copy-done.5, bf16[1536,512]{1,0:T(8,128)(2,1)S(1)} %copy-done.2), kind=kOutput, calls=%fused_computation.32 | convolution fusion | flops 167772160 | bytes 1507328 | tf_op jit(solution)/shard_map/dot_general | solution.py:79
  14.3 1.2 %compare_select_fusion.3 = (s32[32]{0:T(128)S(1)}, s32[32]{0:T(128)}) fusion(s32[32]{0:T(128)} %param.23, s32[]{:T(128)S(6)} %mul.80), kind=kLoop, calls=%fused_computation.58 | loop fusion | flops 128 | bytes 388 | tf_op jit(solution)/shard_map/select_n | solution.py:124
  16.0 1.7 %fusion.14 = f32[32,512]{1,0:T(8,128)} fusion(bf16[32,512]{1,0:T(8,128)(2,1)} %param.21, bf16[1536,512]{1,0:T(8,128)(2,1)S(1)} %copy-done.2), kind=kOutput, calls=%fused_computation.25 | convolution fusion | flops 16777216 | bytes 622592 | tf_op jit(solution)/shard_map/dot_general | solution.py:120
  17.7 1.2 %fusion.35 = s32[32]{0:T(128)} fusion(s32[32]{0:T(128)} %param.22), kind=kLoop, calls=%fused_computation.70 | loop fusion | flops 448 | bytes 256 | tf_op jit(solution)/shard_map/add | solution.py:94
  20.1 0.7 pad_clamp_fusion.3
  20.8 2.0 %fusion.16 = f32[960,512]{1,0:T(8,128)} fusion(bf16[960,512]{1,0:T(8,128)(2,1)S(1)} %copy-done, bf16[1536,512]{1,0:T(8,128)(2,1)S(1)} %copy-done.2), kind=kOutput, calls=%fused_computation.27 | convolution fusion | flops 503316480 | bytes 3473408 | tf_op jit(solution)/shard_map/dot_general | solution.py:90
  23.0 0.7 gather_fusion.3
  23.7 1.3 %pad_add_fusion = s32[992]{0:T(1024)} fusion(s32[32]{0:T(128)} %get-tuple-element.8, s32[960]{0:T(1024)} %get-tuple-element.6), kind=kLoop, calls=%fused_computation.55 | loop fusion | flops 992 | bytes 7936 | tf_op jit(solution)/shard_map/concatenate | solution.py:128
  25.1 5.1 %gather_fusion.2 = f32[960,512]{1,0:T(8,128)} fusion(f32[160,512]{1,0:T(8,128)S(1)} %fusion.10, s32[1024]{0:T(1024)} %pad_clamp_fusion.1), kind=kCustom, calls=%fused_computation.2 | custom fusion | bytes 3936000 | tf_op jit(solution)/shard_map/gather | solution.py:92
  30.1 4.8 %gather_fusion = f32[960,512]{1,0:T(8,128)} fusion(f32[320,512]{1,0:T(8,128)S(1)} %fusion.21, s32[1024]{0:T(1024)S(1)} %pad_clamp_fusion.3), kind=kCustom, calls=%fused_computation | custom fusion | bytes 3936000 | tf_op jit(solution)/shard_map/gather | solution.py:87
  35.0 0.8 %pad_add_fusion.1 = s32[80]{0:T(128)S(1)} fusion(s32[40]{0:T(128)} %bitcast.4, s32[40]{0:T(128)} %bitcast.3), kind=kLoop, calls=%fused_computation.74 | loop fusion | flops 80 | bytes 640 | tf_op jit(solution)/shard_map/concatenate | solution.py:77
  35.9 0.9 %collective-permute-start.5 = (bf16[8,512]{1,0:T(8,128)(2,1)S(1)}, bf16[8,512]{1,0:T(8,128)(2,1)S(1)}, u32[]{:S(2)}, u32[]{:S(2)}) collective-permute-start(bf16[8,512]{1,0:T(8,128)(2,1)S(1)} %pad_maximum_fusion.2), channel_id=1, source_target_pairs={{0,14},{1,15},{2,0},{3,1},{4,2},{5,3},{6,4},{7,5},{8,6},{9,7},{10,... | collective-permute-start | bytes 24584 | tf_op jit(solution)/shard_map/ppermute | solution.py:106
  36.8 3.7 %collective-permute-done.5 = bf16[8,512]{1,0:T(8,128)(2,1)S(1)} collective-permute-done((bf16[8,512]{1,0:T(8,128)(2,1)S(1)}, bf16[8,512]{1,0:T(8,128)(2,1)S(1)}, u32[]{:S(2)}, u32[]{:S(2)}) %collective-permute-start.5) | collective-permute-done | bytes 8224 | tf_op jit(solution)/shard_map/ppermute | solution.py:106
  40.5 3.9 %collective-permute-start.6 = (bf16[16,512]{1,0:T(8,128)(2,1)S(1)}, bf16[16,512]{1,0:T(8,128)(2,1)S(1)}, u32[]{:S(2)}, u32[]{:S(2)}) collective-permute-start(bf16[16,512]{1,0:T(8,128)(2,1)S(1)} %pad_maximum_fusion.1), channel_id=1, source_target_pairs={{0,12},{1,13},{2,14},{3,15},{4,0},{5,1},{6,2},{7,3},{8,4},{9,5},{1... | collective-permute-start | bytes 49160 | tf_op jit(solution)/shard_map/ppermute | solution.py:106
  44.4 1.4 %collective-permute-done.6 = bf16[16,512]{1,0:T(8,128)(2,1)S(1)} collective-permute-done((bf16[16,512]{1,0:T(8,128)(2,1)S(1)}, bf16[16,512]{1,0:T(8,128)(2,1)S(1)}, u32[]{:S(2)}, u32[]{:S(2)}) %collective-permute-start.6) | collective-permute-done | bytes 16416 | tf_op jit(solution)/shard_map/ppermute | solution.py:106
  46.5 4.7 %collective-permute-start.7 = (bf16[32,512]{1,0:T(8,128)(2,1)}, bf16[32,512]{1,0:T(8,128)(2,1)}, u32[]{:S(2)}, u32[]{:S(2)}) collective-permute-start(bf16[32,512]{1,0:T(8,128)(2,1)} %pad_maximum_fusion), channel_id=1, source_target_pairs={{0,8},{1,9},{2,10},{3,11},{4,12},{5,13},{6,14},{7,15},{8,0},{9,1},... | collective-permute-start | bytes 98312 | tf_op jit(solution)/shard_map/ppermute | solution.py:106
  51.2 1.3 %fusion.19 = f32[80,512]{1,0:T(8,128)S(1)} fusion(bf16[1536,512]{1,0:T(8,128)(2,1)} %param.24, bf16[40,512]{1,0:T(8,128)(2,1)} %bitcast.2, bf16[40,512]{1,0:T(8,128)(2,1)} %bitcast.1), kind=kOutput, calls=%fused_computation.30 | convolution fusion | flops 42106880 | bytes 770048 | tf_op jit(solution)/shard_map/dot_general | solution.py:80
  52.5 4.9 %gather_fusion.1 = f32[960,512]{1,0:T(8,128)} fusion(f32[80,512]{1,0:T(8,128)S(1)} %fusion.19, s32[1024]{0:T(1024)S(1)} %pad_clamp_fusion.2), kind=kCustom, calls=%fused_computation.1 | custom fusion | bytes 3936000 | tf_op jit(solution)/shard_map/gather | solution.py:87
  57.4 4.4 %add_add_fusion = f32[960,512]{1,0:T(8,128)} fusion(f32[960,512]{1,0:T(8,128)} %gather_fusion.2, f32[960,512]{1,0:T(8,128)S(1)} %copy-done.1, f32[960,512]{1,0:T(8,128)} %gather_fusion, f32[960,512]{1,0:T(8,128)} %gather_fusion.1, pred[960]{0:T(1024)(128)(4,1)S(1)} %copy-done.9), kind=kLoop, calls=%fused_computation.8 | loop fusion | flops 1474560 | bytes 9831360 | tf_op jit(solution)/shard_map/add | solution.py:90
  61.8 1.6 %concatenate.36 = bf16[128,512]{1,0:T(8,128)(2,1)S(1)} concatenate(bf16[4,512]{1,0:T(4,128)(2,1)S(1)} %slice.26, bf16[4,512]{1,0:T(4,128)(2,1)S(1)} %collective-permute-done.4, bf16[8,512]{1,0:T(8,128)(2,1)S(1)} %collective-permute-done.5, bf16[16,512]{1,0:T(8,128)(2,1)S(1)} %collective-permute-done.6, bf16[32,512]{1,0:T(8,128)(2,1)} %collective-permute-done.7, ...), dimensions={0} | concatenate | bytes 262144 | tf_op jit(solution)/shard_map/jit(_roll_dynamic)/concatenate | solution.py:113
  63.4 2.0 %fusion.1 = f32[32,512]{1,0:T(8,128)} fusion(f32[32,512]{1,0:T(8,128)S(1)} %gather_fusion.3, f32[32,512]{1,0:T(8,128)S(1)} %copy-done.6, bf16[1536,512]{1,0:T(8,128)(2,1)} %param.24, bf16[128,512]{1,0:T(8,128)(2,1)S(1)} %concatenate.36, s32[]{:T(128)S(6)} %select_n.86, s32[32]{0:T(128)S(1)} %copy-done.14), kind=kOutput, calls=%fused_computation.13 | convolution fusion | flops 18925568 | bytes 786948 | tf_op jit(solution)/shard_map/dot_general | solution.py:123
  65.4 2.5 %fusion.44 = (f32[992]{0:T(1024)S(1)}, f32[992,512]{1,0:T(8,128)S(1)}) fusion(bf16[512,512]{1,0:T(8,128)(2,1)} %param.26, f32[32,512]{1,0:T(8,128)} %fusion.1, f32[960,512]{1,0:T(8,128)} %add_add_fusion, f32[512]{0:T(512)S(1)} %copy-done.15), kind=kOutput, calls=%fused_computation.81 | convolution fusion | flops 524155936 | bytes 4593536 | tf_op jit(solution)/shard_map/dot_general | solution.py:30
  68.6 2.6 %multiply_convert_fusion.2 = bf16[160,512]{1,0:T(8,128)(2,1)} fusion(f32[160,512]{1,0:T(8,128)S(1)} %fusion.12, bf16[1024,512]{1,0:T(8,128)(2,1)} %param.29, f32[992,512]{1,0:T(8,128)S(1)} %get-tuple-element.10, f32[512]{0:T(512)S(1)} %copy-done.16, f32[512]{0:T(512)S(1)} %copy-done.17, f32[992]{0:T(1024)S(1)} %add_rsqrt_fusion, ...), kind=kOutput, calls=%fused_computation.36 | convolution fusion | flops 249768960 | bytes 3065472 | tf_op jit(solution)/shard_map/dot_general | solution.py:135
  71.2 1.5 %fusion.45 = (f32[160]{0:T(256)S(1)}, f32[160,512]{1,0:T(8,128)S(1)}) fusion(bf16[160,512]{1,0:T(8,128)(2,1)} %multiply_convert_fusion.2, bf16[512,512]{1,0:T(8,128)(2,1)} %param.31), kind=kOutput, calls=%fused_computation.82 | convolution fusion | flops 83967840 | bytes 1016448 | tf_op jit(solution)/shard_map/dot_general | solution.py:30
  73.0 0.8 %add_convert_fusion.3 = bf16[160,512]{1,0:T(8,128)(2,1)} fusion(bf16[160,512]{1,0:T(8,128)(2,1)S(1)} %copy-done.4, f32[160,512]{1,0:T(8,128)S(1)} %get-tuple-element.12, f32[512]{0:T(512)S(1)} %copy-done.12, f32[512]{0:T(512)S(1)} %copy-done.13, f32[160]{0:T(256)S(1)} %add_rsqrt_fusion.1, f32[160]{0:T(256)S(1)} %broadcast_multiply_fusion.1), kind=kLoop, calls=%fused_computation.34 | loop fusion | flops 573440 | bytes 660736 | tf_op jit(solution)/shard_map/convert_element_type | solution.py:140
  (66 shorter events, 6.5 us)
Async XLA Ops:
  0.0 20.8 %copy-start = (bf16[960,512]{1,0:T(8,128)(2,1)S(1)}, bf16[960,512]{1,0:T(8,128)(2,1)}, u32[]{:S(2)}) copy-start(bf16[960,512]{1,0:T(8,128)(2,1)} %param.18) | copy-start | bytes 2949124
  0.0 11.8 %copy-start.2 = (bf16[1536,512]{1,0:T(8,128)(2,1)S(1)}, bf16[1536,512]{1,0:T(8,128)(2,1)}, u32[]{:S(2)}) copy-start(bf16[1536,512]{1,0:T(8,128)(2,1)} %param.24) | copy-start | bytes 4718596
  0.0 13.1 %copy-start.8 = (s32[960]{0:T(1024)S(1)}, s32[960]{0:T(1024)}, u32[]{:S(2)}) copy-start(s32[960]{0:T(1024)} %param.19) | copy-start | bytes 11524
  0.0 18.9 %copy-start.10 = (s32[960]{0:T(1024)S(1)}, s32[960]{0:T(1024)}, u32[]{:S(2)}) copy-start(s32[960]{0:T(1024)} %param.20) | copy-start | bytes 11524
  0.5 34.4 %collective-permute-start.2 = (s32[1,40]{1,0:T(1,128)}, s32[1,40]{1,0:T(1,128)}, u32[]{:S(2)}, u32[]{:S(2)}) collective-permute-start(s32[1,40]{1,0:T(1,128)} %fusion.34), channel_id=1, source_target_pairs={{0,2},{2,4},{4,6},{6,8},{8,10},{10,12},{12,14},{14,0},{1,3},{3,5},... | collective-permute-start | bytes 488 | tf_op jit(solution)/shard_map/ppermute | solution.py:16
  2.1 32.9 %collective-permute-start.3 = (s32[1,40]{1,0:T(1,128)}, s32[1,40]{1,0:T(1,128)}, u32[]{:S(2)}, u32[]{:S(2)}) collective-permute-start(s32[1,40]{1,0:T(1,128)} %fusion.34), channel_id=1, source_target_pairs={{2,0},{4,2},{6,4},{8,6},{10,8},{12,10},{14,12},{0,14},{3,1},{5,3},... | collective-permute-start | bytes 488 | tf_op jit(solution)/shard_map/ppermute | solution.py:17
  4.8 0.7 copy-start.5
  6.2 45.0 %collective-permute-start = (bf16[1,40,512]{2,1,0:T(8,128)(2,1)}, bf16[1,40,512]{2,1,0:T(8,128)(2,1)}, u32[]{:S(2)}, u32[]{:S(2)}) collective-permute-start(bf16[1,40,512]{2,1,0:T(8,128)(2,1)} %broadcast_in_dim_reshape.3), channel_id=1, source_target_pairs={{0,2},{2,4},{4,6},{6,8},{8,10},{10,12},{12,14},{14,0},{1,3},{3,5},... | collective-permute-start | bytes 122888 | tf_op jit(solution)/shard_map/ppermute | solution.py:16
  8.6 42.6 %collective-permute-start.1 = (bf16[1,40,512]{2,1,0:T(8,128)(2,1)}, bf16[1,40,512]{2,1,0:T(8,128)(2,1)}, u32[]{:S(2)}, u32[]{:S(2)}) collective-permute-start(bf16[1,40,512]{2,1,0:T(8,128)(2,1)} %broadcast_in_dim_reshape.3), channel_id=1, source_target_pairs={{2,0},{4,2},{6,4},{8,6},{10,8},{12,10},{14,12},{0,14},{3,1},{5,3},... | collective-permute-start | bytes 122888 | tf_op jit(solution)/shard_map/ppermute | solution.py:17
  9.3 26.5 %collective-permute-start.4 = (bf16[4,512]{1,0:T(4,128)(2,1)S(1)}, bf16[4,512]{1,0:T(4,128)(2,1)S(1)}, u32[]{:S(2)}, u32[]{:S(2)}) collective-permute-start(bf16[4,512]{1,0:T(4,128)(2,1)S(1)} %slice.26), channel_id=1, source_target_pairs={{0,15},{1,0},{2,1},{3,2},{4,3},{5,4},{6,5},{7,6},{8,7},{9,8},{10,9... | collective-permute-start | bytes 12296 | tf_op jit(solution)/shard_map/ppermute | solution.py:106
  16.0 6.7 %copy-start.3 = (bf16[160,512]{1,0:T(8,128)(2,1)S(1)}, bf16[160,512]{1,0:T(8,128)(2,1)}, u32[]{:S(2)}) copy-start(bf16[160,512]{1,0:T(8,128)(2,1)} %param.17) | copy-start | bytes 491524
  16.0 6.7 %copy-start.7 = (bf16[1024,512]{1,0:T(8,128)(2,1)S(1)}, bf16[1024,512]{1,0:T(8,128)(2,1)}, u32[]{:S(2)}) copy-start(bf16[1024,512]{1,0:T(8,128)(2,1)} %param.29) | copy-start | bytes 3145732
  35.9 4.6 %collective-permute-start.5 = (bf16[8,512]{1,0:T(8,128)(2,1)S(1)}, bf16[8,512]{1,0:T(8,128)(2,1)S(1)}, u32[]{:S(2)}, u32[]{:S(2)}) collective-permute-start(bf16[8,512]{1,0:T(8,128)(2,1)S(1)} %pad_maximum_fusion.2), channel_id=1, source_target_pairs={{0,14},{1,15},{2,0},{3,1},{4,2},{5,3},{6,4},{7,5},{8,6},{9,7},{10,... | collective-permute-start | bytes 24584 | tf_op jit(solution)/shard_map/ppermute | solution.py:106
  40.5 5.4 %collective-permute-start.6 = (bf16[16,512]{1,0:T(8,128)(2,1)S(1)}, bf16[16,512]{1,0:T(8,128)(2,1)S(1)}, u32[]{:S(2)}, u32[]{:S(2)}) collective-permute-start(bf16[16,512]{1,0:T(8,128)(2,1)S(1)} %pad_maximum_fusion.1), channel_id=1, source_target_pairs={{0,12},{1,13},{2,14},{3,15},{4,0},{5,1},{6,2},{7,3},{8,4},{9,5},{1... | collective-permute-start | bytes 49160 | tf_op jit(solution)/shard_map/ppermute | solution.py:106
  46.5 15.4 %collective-permute-start.7 = (bf16[32,512]{1,0:T(8,128)(2,1)}, bf16[32,512]{1,0:T(8,128)(2,1)}, u32[]{:S(2)}, u32[]{:S(2)}) collective-permute-start(bf16[32,512]{1,0:T(8,128)(2,1)} %pad_maximum_fusion), channel_id=1, source_target_pairs={{0,8},{1,9},{2,10},{3,11},{4,12},{5,13},{6,14},{7,15},{8,0},{9,1},... | collective-permute-start | bytes 98312 | tf_op jit(solution)/shard_map/ppermute | solution.py:106
  52.5 4.9 %copy-start.1 = (f32[960,512]{1,0:T(8,128)S(1)}, f32[960,512]{1,0:T(8,128)}, u32[]{:S(2)}) copy-start(f32[960,512]{1,0:T(8,128)} %fusion.16) | copy-start | bytes 5898244
  52.5 4.9 %copy-start.9 = (pred[960]{0:T(1024)(128)(4,1)S(1)}, pred[960]{0:T(1024)(128)(4,1)}, u32[]{:S(2)}) copy-start(pred[960]{0:T(1024)(128)(4,1)} %compare_and_fusion) | copy-start | bytes 2884
  57.4 6.0 %copy-start.6 = (f32[32,512]{1,0:T(8,128)S(1)}, f32[32,512]{1,0:T(8,128)}, u32[]{:S(2)}) copy-start(f32[32,512]{1,0:T(8,128)} %fusion.14) | copy-start | bytes 196612
  57.4 6.0 %copy-start.14 = (s32[32]{0:T(128)S(1)}, s32[32]{0:T(128)}, u32[]{:S(2)}) copy-start(s32[32]{0:T(128)} %fusion.35) | copy-start | bytes 388
  57.4 8.1 %copy-start.15 = (f32[512]{0:T(512)S(1)}, f32[512]{0:T(512)}, u32[]{:S(2)}) copy-start(f32[512]{0:T(512)} %param.25) | copy-start | bytes 6148
  67.9 0.7 copy-start.11
  67.9 0.7 copy-start.16
  67.9 0.7 copy-start.17
  67.9 0.7 copy-start.18
  68.6 4.3 %copy-start.4 = (bf16[160,512]{1,0:T(8,128)(2,1)S(1)}, bf16[160,512]{1,0:T(8,128)(2,1)}, u32[]{:S(2)}) copy-start(bf16[160,512]{1,0:T(8,128)(2,1)} %param.17) | copy-start | bytes 491524
  68.6 4.3 %copy-start.12 = (f32[512]{0:T(512)S(1)}, f32[512]{0:T(512)}, u32[]{:S(2)}) copy-start(f32[512]{0:T(512)} %param.33) | copy-start | bytes 6148
  68.6 4.3 %copy-start.13 = (f32[512]{0:T(512)S(1)}, f32[512]{0:T(512)}, u32[]{:S(2)}) copy-start(f32[512]{0:T(512)} %param.32) | copy-start | bytes 6148
